TPU v7x, 256 devices: a whole 4x4x8 slice. The times are simulated.
256 devices in a mesh: row: 16 (over y, x), col: 16 (over z, core).
Axes of the slice: x: 4, y: 4, z: 8, core: 2. Of those that a mesh axis runs over, the one named last changes fastest.
Arguments:
- panel: bfloat16 [15, 32, 512, 512], P(None, 'row', 'col'), may hold values from -0.109375 to 0.109375
- diag_inverse: float32 [6, 32, 512, 512], P(None, 'row', 'col'), as said below
- parents: int32 [5, 32], replicated, may hold values from 0 to 31, as said below
- supernode_sizes: int32 [6, 32], replicated, may hold values from 128 to 512
Outputs:
- cross: float32 [15, 32, 512, 512], P(None, 'row', 'col')
- marginal: float32 [6, 32, 512, 512], P(None, 'row', 'col')
Inputs may be any that keep to these rules, and one draw needn't show every extreme that they name: `parents`: the parent of a supernode g of level d + 1 is a supernode of level d whose index divided by 2 equals g divided by 2, or that minus 1 modulo 32 / 2. `diag_inverse`: every block is symmetric and positive definite.
All inputs are finite; a program needn't handle non-finite values.
Results may differ from a plain program's by a relative error of at most 0.0023.
Values may be sent and summed in bfloat16 or wider, within the bound.
A program may use at most 128 MiB of HBM per device.

v0:
```python
import jax
import jax.numpy as jnp
from jax import lax
from jax.sharding import PartitionSpec as P


def from_behind(x, axis, by):
    size = lax.axis_size(axis)
    return lax.ppermute(x, axis, [(i, (i + by) % size) for i in range(size)])


def turn_over(cross):
    swapped = lax.all_to_all(cross, "col", split_axis=3, concat_axis=2, tiled=True)
    return jnp.swapaxes(swapped, 2, 3)


def shards(panel, diag_inverse, parents, supernode_sizes):
    levels = diag_inverse.shape[0]
    per_row = diag_inverse.shape[1]
    row_count = diag_inverse.shape[2]
    width = diag_inverse.shape[3]
    my_row = lax.axis_index("row")
    my_col = lax.axis_index("col")
    my_nodes = my_row * per_row + jnp.arange(per_row, dtype=jnp.int32)
    my_lines = my_col * row_count + jnp.arange(row_count, dtype=jnp.int32)
    columns = jnp.arange(width, dtype=jnp.int32)
    on_diag = (my_lines[:, None] == columns[None, :]).astype(jnp.float32)
    ancestry_ids = jnp.zeros((0, parents.shape[1]), jnp.int32)
    crosses = []
    diagonals = []
    chain = None
    for level in range(levels):
        own_sizes = supernode_sizes[level][my_nodes]
        live_cols = (columns[None, :] < own_sizes[:, None]).astype(jnp.float32)
        live_lines = (my_lines[None, :] < own_sizes[:, None]).astype(jnp.float32)
        diag_base = (
            diag_inverse[level] * live_lines[:, :, None] * live_cols[:, None, :]
            + on_diag[None] * (1.0 - live_lines)[:, :, None]
        )
        if level == 0:
            diagonal = diag_base
        else:
            parent_ids = parents[level - 1]
            ancestry_ids = jnp.concatenate(
                [ancestry_ids[:, parent_ids], parent_ids[None, :]], axis=0
            )
            my_parents = parent_ids[my_nodes]
            pick_slot = jnp.where(
                my_parents // per_row == my_row,
                my_parents % per_row,
                per_row + my_parents % per_row,
            )
            passed = from_behind(chain, "row", 1)
            ancestry = jnp.take(jnp.concatenate([chain, passed], axis=0), pick_slot, axis=0)
            upper_sizes = supernode_sizes[
                jnp.arange(level, dtype=jnp.int32)[:, None], ancestry_ids[:, my_nodes]
            ]
            live_upper = (my_lines[None, None, :] < upper_sizes[:, :, None]).astype(jnp.float32)
            start = level * (level - 1) // 2
            keep = (live_upper[:, :, :, None] * live_cols[None, :, None, :]).astype(jnp.bfloat16)
            lower = jnp.transpose(panel[start : start + level] * keep, (1, 0, 2, 3))
            whole = lax.all_gather(lower, "col", axis=2, tiled=True).astype(jnp.float32)
            cross = -jnp.einsum(
                "nlmik,nmkj->nlij", ancestry, whole, precision=lax.Precision.HIGHEST
            )
            turned = turn_over(cross)
            diagonal = diag_base - jnp.einsum(
                "nlik,nlkj->nij", turned, whole, precision=lax.Precision.HIGHEST
            )
            crosses.append(jnp.transpose(cross, (1, 0, 2, 3)))
        diagonals.append(diagonal)
        if level < levels - 1:
            if level == 0:
                chain = diagonal[:, None, None]
            else:
                upper = jnp.concatenate([ancestry, cross[:, :, None]], axis=2)
                bottom = jnp.concatenate([turned[:, None], diagonal[:, None, None]], axis=2)
                chain = jnp.concatenate([upper, bottom], axis=1)
    return (jnp.concatenate(crosses, axis=0), jnp.stack(diagonals))


def solution(mesh):
    in_specs = (P(None, "row", "col", None), P(None, "row", "col", None), P(), P())
    out_specs = (P(None, "row", "col", None), P(None, "row", "col", None))
    return jax.shard_map(shards, mesh=mesh, in_specs=in_specs, out_specs=out_specs, check_vma=False)
```

profile of v0, /device:TPU:1, one launch (start us, length us, event | category | flops | bytes accessed | tf_op | source)
XLA Modules:
  0.0 466.2 jit_solution(5601063711213045064)
XLA Ops:
  26.2 2.1 collective-permute-start
  28.4 6.0 %collective-permute-done = f32[2,1,1,32,512]{4,3,0,2,1:T(8,128)S(1)} collective-permute-done((f32[2,1,1,32,512]{4,3,0,2,1:T(8,128)S(1)}, f32[2,1,1,32,512]{4,3,0,2,1:T(8,128)S(1)}, u32[]{:S(2)}, u32[]{:S(2)}) %collective-permute-start) | collective-permute-done | bytes 131104 | tf_op jit(solution)/shard_map/ppermute | solution.py:9
  35.0 23.7 %all-gather.15.cloned.1.call-done = bf16[1,2,512,512]{3,2,1,0:T(8,128)(2,1)} async-done(((bf16[1,2,32,512]{3,2,1,0:T(8,128)(2,1)}), bf16[1,2,512,512]{3,2,1,0:T(8,128)(2,1)}) %all-gather.15.cloned.1.call-update) | async-done | bytes 1048592 | tf_op jit(solution)/shard_map/all_gather | solution.py:62
  58.7 2.6 bitcast_dynamic-update-slice_fusion.4
  62.7 4.7 all-to-all-start
  68.8 7.5 %all-to-all-done = f32[16,1,2048]{2,1,0:T(1,128)S(1)} async-done(((f32[16,1,2048]{2,1,0:T(1,128)}), f32[16,1,2048]{2,1,0:T(1,128)S(1)}, u32[]{:S(2)}, u32[]{:S(2)}) %all-to-all-start) | async-done | bytes 131104 | tf_op jit(solution)/shard_map/all_to_all | solution.py:13
  81.4 15.8 %collective-permute-done.1 = f32[2,2,2,32,512]{4,3,0,2,1:T(8,128)S(1)} collective-permute-done((f32[2,2,2,32,512]{4,3,0,2,1:T(8,128)S(1)}, f32[2,2,2,32,512]{4,3,0,2,1:T(8,128)S(1)}, u32[]{:S(2)}, u32[]{:S(2)}) %collective-permute-start.1) | collective-permute-done | bytes 524320 | tf_op jit(solution)/shard_map/ppermute | solution.py:9
  99.0 3.5 bitcast_dynamic-update-slice_fusion.3
  105.0 4.5 all-to-all-start.1
  112.4 11.4 %all-to-all-done.1 = f32[16,1,4096]{2,1,0:T(1,128)S(1)} async-done(((f32[16,1,4096]{2,1,0:T(1,128)}), f32[16,1,4096]{2,1,0:T(1,128)S(1)}, u32[]{:S(2)}, u32[]{:S(2)}) %all-to-all-start.1) | async-done | bytes 262176 | tf_op jit(solution)/shard_map/all_to_all | solution.py:13
  126.9 2.9 copy.212
  131.4 2.7 bitcast_dynamic-update-slice_fusion.7
  138.1 27.5 %collective-permute-done.2 = f32[2,3,3,32,512]{4,3,2,1,0:T(8,128)} collective-permute-done((f32[2,3,3,32,512]{4,3,2,1,0:T(8,128)S(1)}, f32[2,3,3,32,512]{4,3,2,1,0:T(8,128)}, u32[]{:S(2)}, u32[]{:S(2)}) %collective-permute-start.2) | collective-permute-done | bytes 1179680 | tf_op jit(solution)/shard_map/ppermute | solution.py:9
  165.6 3.0 pad_maximum_fusion.2
  168.6 2.3 gather_fusion.12
  171.2 4.3 bitcast_dynamic-update-slice_fusion.2
  176.6 2.3 reshape.1603
  178.9 18.5 %all_to_all.90 = f32[16,1,6144]{2,1,0:T(1,128)S(1)} all-to-all(f32[16,1,6144]{2,1,0:T(1,128)} %reshape.1603), channel_id=1, replica_groups=mesh['row'=16,'col'=16] {'col'}, dimensions={0} | all-to-all | bytes 786432 | tf_op jit(solution)/shard_map/all_to_all | solution.py:13
  197.4 2.4 reduce.8
  199.8 2.3 reshape.1604
  202.1 2.1 copy.211
  206.2 4.1 bitcast_dynamic-update-slice_fusion.6
  212.6 50.1 %collective-permute-done.3 = f32[2,4,4,32,512]{4,3,2,1,0:T(8,128)} collective-permute-done((f32[2,4,4,32,512]{4,3,2,1,0:T(8,128)}, f32[2,4,4,32,512]{4,3,2,1,0:T(8,128)}, u32[]{:S(2)}, u32[]{:S(2)}) %collective-permute-start.3) | collective-permute-done | bytes 2097184 | tf_op jit(solution)/shard_map/ppermute | solution.py:9
  262.7 4.2 pad_maximum_fusion.1
  266.9 4.2 gather_fusion.18
  273.1 4.8 %bitcast_dynamic-update-slice_fusion.1 = (f32[15,2,32,512]{3,2,0,1:T(8,128)}, f32[2,4,32,512]{3,2,1,0:T(8,128)S(1)}) fusion(f32[15,2,32,512]{3,2,0,1:T(8,128)} %get-tuple-element.48, f32[2,4,4,32,512]{4,3,2,1,0:T(8,128)S(1)} %broadcast_select_fusion, bf16[2,4,512,512]{3,2,1,0:T(8,128)(2,1)} %all-gather.11.cloned.1.call-done), kind=kOutput, calls=%fused_computation.81 | convolution fusion | flops 3221356544 | bytes 7340032 | tf_op jit(solution)/shard_map/nlmik,nmkj->nlij/dot_general | solution.py:63
  279.7 2.8 reshape.1605
  282.6 21.0 %all_to_all.91 = f32[16,1,8192]{2,1,0:T(1,128)} all-to-all(f32[16,1,8192]{2,1,0:T(1,128)S(1)} %reshape.1605), channel_id=1, replica_groups=mesh['row'=16,'col'=16] {'col'}, dimensions={0} | all-to-all | bytes 1048576 | tf_op jit(solution)/shard_map/all_to_all | solution.py:13
  303.6 2.9 reduce.9
  306.5 2.5 reshape.1606
  309.0 4.1 copy.210
  313.1 2.3 all_to_all.80
  315.4 4.9 %bitcast_dynamic-update-slice_fusion.5 = (f32[6,2,32,512]{3,2,1,0:T(8,128)}, f32[2,32,512]{2,1,0:T(8,128)S(1)}) fusion(f32[6,2,32,512]{3,2,1,0:T(8,128)} %get-tuple-element.58, bf16[2,4,512,512]{3,2,1,0:T(8,128)(2,1)} %all-gather.11.cloned.1.call-done, f32[2,4,512,32]{2,3,1,0:T(8,128)S(1)} %all_to_all.80, f32[2,32]{1,0:T(2,128)S(1)} %get-tuple-element.39, ...), kind=kOutput, calls=%fused_computation.105 | convolution fusion | flops 805470208 | bytes 5181952 | tf_op jit(solution)/shard_map/nlik,nlkj->nij/dot_general | solution.py:67
  320.4 2.1 maximum_maximum_fusion
  323.4 74.8 %collective-permute-done.4 = f32[2,5,5,32,512]{4,3,2,1,0:T(8,128)} collective-permute-done((f32[2,5,5,32,512]{4,3,2,1,0:T(8,128)}, f32[2,5,5,32,512]{4,3,2,1,0:T(8,128)}, u32[]{:S(2)}, u32[]{:S(2)}) %collective-permute-start.4) | collective-permute-done | bytes 3276832 | tf_op jit(solution)/shard_map/ppermute | solution.py:9
  398.2 4.7 %pad_maximum_fusion = f32[4,5,5,32,512]{4,3,2,1,0:T(8,128)} fusion(f32[2,5,5,32,512]{4,3,2,1,0:T(8,128)} %collective-permute-done.4, f32[2,1,1,32,512]{4,3,2,1,0:T(8,128)S(1)} %bitcast.445, f32[2,1,4,32,512]{4,3,2,1,0:T(8,128)S(1)} %bitcast.421, f32[2,4,1,32,512]{4,3,2,1,0:T(8,128)S(1)} %bitcast.436, f32[2,4,4,32,512]{4,3,2,1,0:T(8,128)S(1)} %broadcast_select_fusion), kind=kLoop, calls=%fused_computation.30 | loop fusion | flops 6553600 | bytes 13107200 | tf_op jit(solution)/shard_map/concatenate | solution.py:54
  402.9 3.6 gather_fusion.24
  406.6 6.4 %bitcast_dynamic-update-slice_fusion = (f32[15,2,32,512]{3,2,0,1:T(8,128)}, f32[2,5,32,512]{3,2,1,0:T(8,128)}) fusion(f32[15,2,32,512]{3,2,0,1:T(8,128)} %get-tuple-element.50, bf16[2,5,512,512]{3,2,1,0:T(8,128)(2,1)} %all-gather.13.cloned.1.call-done, f32[2,5,5,32,512]{4,3,2,1,0:T(8,128)S(1)} %gather_fusion.24, pred[2]{0:T(512)(128)(4,1)S(1)} %compare_and_fusion), kind=kOutput, calls=%fused_computation.76 | convolution fusion | flops 5034147840 | bytes 9830402 | tf_op jit(solution)/shard_map/nlmik,nmkj->nlij/dot_general | solution.py:63
  412.9 3.1 copy.173
  416.0 3.4 reshape.1607
  419.4 4.3 all-to-all-start.4
  423.7 3.1 copy.175
  426.8 16.8 %all-to-all-done.4 = f32[16,1,10240]{2,1,0:T(1,128)S(1)} async-done(((f32[16,1,10240]{2,1,0:T(1,128)}), f32[16,1,10240]{2,1,0:T(1,128)S(1)}, u32[]{:S(2)}, u32[]{:S(2)}) %all-to-all-start.4) | async-done | bytes 655392 | tf_op jit(solution)/shard_map/all_to_all | solution.py:13
  443.5 2.2 reduce.10
  445.7 2.2 reshape.1608
  447.9 3.1 copy.209
  451.0 2.5 all_to_all.84
  453.5 5.7 %fusion.43 = f32[6,2,32,512]{3,2,1,0:T(8,128)} fusion(f32[6,2,32,512]{3,2,1,0:T(8,128)} %get-tuple-element.60, bf16[2,5,512,512]{3,2,1,0:T(8,128)(2,1)} %all-gather.13.cloned.1.call-done, f32[2,5,512,32]{2,3,1,0:T(8,128)S(1)} %all_to_all.84, f32[6,2,32,512]{3,2,1,0:T(8,128)} %param.5, f32[2,32]{1,0:T(2,128)S(1)} %get-tuple-element.38, ...), kind=kOutput, calls=%fused_computation.67 | convolution fusion | flops 1006796800 | bytes 6230528 | tf_op jit(solution)/shard_map/nlik,nlkj->nij/dot_general | solution.py:67
  (155 shorter events, 53.7 us)
Async XLA Ops:
  7.2 8.7 %copy-start.5 = (s32[5,32]{1,0:T(8,128)S(1)}, s32[5,32]{1,0:T(8,128)}, u32[]{:S(2)}) copy-start(s32[5,32]{1,0:T(8,128)} %param.6) | copy-start | bytes 1924
  7.2 7.9 %copy-start.4 = (bf16[15,2,32,512]{3,2,1,0:T(8,128)(2,1)S(1)}, bf16[15,2,32,512]{3,2,1,0:T(8,128)(2,1)}, u32[]{:S(2)}) copy-start(bf16[15,2,32,512]{3,2,1,0:T(8,128)(2,1)} %param.4) | copy-start | bytes 2949124
  7.2 51.5 %all-gather.15.cloned.1.call-start = ((), (), s32[]{:S(2)}) async-start(), calls=%async_computation.9 | async-start | bytes 1114112 | tf_op jit(solution)/shard_map/all_gather | solution.py:62
  8.8 8.6 %copy-start = (s32[6,32]{1,0:T(8,128)S(1)}, s32[6,32]{1,0:T(8,128)}, u32[]{:S(2)}) copy-start(s32[6,32]{1,0:T(8,128)} %param.7) | copy-start | bytes 2308
  15.8 83.2 %all-gather.7.cloned.1.call-start = ((), (), s32[]{:S(2)}) async-start(), calls=%async_computation.5 | async-start | bytes 2228224 | tf_op jit(solution)/shard_map/all_gather | solution.py:62
  19.2 152.0 %all-gather.9.cloned.1.call-start = ((), (), s32[]{:S(2)}) async-start(), calls=%async_computation.6 | async-start | bytes 3342336 | tf_op jit(solution)/shard_map/all_gather | solution.py:62
  21.3 4.8 %copy-start.3 = (f32[6,2,32,512]{3,2,1,0:T(8,128)S(1)}, f32[6,2,32,512]{3,2,1,0:T(8,128)}, u32[]{:S(2)}) copy-start(f32[6,2,32,512]{3,2,1,0:T(8,128)} %param.5) | copy-start | bytes 2359300
  22.5 250.6 %all-gather.11.cloned.1.call-start = ((), (), s32[]{:S(2)}) async-start(), calls=%async_computation.7 | async-start | bytes 4456448 | tf_op jit(solution)/shard_map/all_gather | solution.py:62
  26.2 8.2 %collective-permute-start = (f32[2,1,1,32,512]{4,3,0,2,1:T(8,128)S(1)}, f32[2,1,1,32,512]{4,3,0,2,1:T(8,128)S(1)}, u32[]{:S(2)}, u32[]{:S(2)}) collective-permute-start(f32[2,1,1,32,512]{4,3,0,2,1:T(8,128)S(1)} %fusion.71), channel_id=1, source_target_pairs={{0,16},{16,32},{32,48},{48,64},{64,80},{80,96},{96,112},{112,128},... | collective-permute-start | bytes 393224 | tf_op jit(solution)/shard_map/ppermute | solution.py:9
  61.5 17.3 %copy-start.2 = (bf16[1,2,512,512]{3,2,1,0:T(8,128)(2,1)S(1)}, bf16[1,2,512,512]{3,2,1,0:T(8,128)(2,1)}, u32[]{:S(2)}) copy-start(bf16[1,2,512,512]{3,2,1,0:T(8,128)(2,1)} %all-gather.15.cloned.1.call-done) | copy-start | bytes 3145732
  62.7 13.6 %all-to-all-start = ((f32[16,1,2048]{2,1,0:T(1,128)}), f32[16,1,2048]{2,1,0:T(1,128)S(1)}, u32[]{:S(2)}, u32[]{:S(2)}) async-start(f32[16,1,2048]{2,1,0:T(1,128)} %reshape.1599), calls=%async_computation | async-start | bytes 262144 | tf_op jit(solution)/shard_map/all_to_all | solution.py:13
  80.1 17.1 %collective-permute-start.1 = (f32[2,2,2,32,512]{4,3,0,2,1:T(8,128)S(1)}, f32[2,2,2,32,512]{4,3,0,2,1:T(8,128)S(1)}, u32[]{:S(2)}, u32[]{:S(2)}) collective-permute-start(f32[2,2,2,32,512]{4,3,0,2,1:T(8,128)S(1)} %maximum_maximum_fusion.3), channel_id=1, source_target_pairs={{0,16},{16,32},{32,48},{48,64},{64,80},{80,96},{96,112},{112,128},... | collective-permute-start | bytes 1572872 | tf_op jit(solution)/shard_map/ppermute | solution.py:9
  105.0 18.8 %all-to-all-start.1 = ((f32[16,1,4096]{2,1,0:T(1,128)}), f32[16,1,4096]{2,1,0:T(1,128)S(1)}, u32[]{:S(2)}, u32[]{:S(2)}) async-start(f32[16,1,4096]{2,1,0:T(1,128)} %reshape.1601), calls=%async_computation.1 | async-start | bytes 524288 | tf_op jit(solution)/shard_map/all_to_all | solution.py:13
  109.5 297.0 %all-gather.13.cloned.1.call-start = ((), (), s32[]{:S(2)}) async-start(), calls=%async_computation.8 | async-start | bytes 5570560 | tf_op jit(solution)/shard_map/all_gather | solution.py:62
  125.0 6.4 %copy-start.1 = (bf16[2,2,512,512]{3,2,1,0:T(8,128)(2,1)S(1)}, bf16[2,2,512,512]{3,2,1,0:T(8,128)(2,1)}, u32[]{:S(2)}) copy-start(bf16[2,2,512,512]{3,2,1,0:T(8,128)(2,1)} %all-gather.7.cloned.1.call-done) | copy-start | bytes 6291460
  134.2 31.4 %collective-permute-start.2 = (f32[2,3,3,32,512]{4,3,2,1,0:T(8,128)S(1)}, f32[2,3,3,32,512]{4,3,2,1,0:T(8,128)}, u32[]{:S(2)}, u32[]{:S(2)}) collective-permute-start(f32[2,3,3,32,512]{4,3,2,1,0:T(8,128)S(1)} %maximum_maximum_fusion.2), channel_id=1, source_target_pairs={{0,16},{16,32},{32,48},{48,64},{64,80},{80,96},{96,112},{112,128},... | collective-permute-start | bytes 3538952 | tf_op jit(solution)/shard_map/ppermute | solution.py:9
  211.9 50.8 %collective-permute-start.3 = (f32[2,4,4,32,512]{4,3,2,1,0:T(8,128)}, f32[2,4,4,32,512]{4,3,2,1,0:T(8,128)}, u32[]{:S(2)}, u32[]{:S(2)}) collective-permute-start(f32[2,4,4,32,512]{4,3,2,1,0:T(8,128)} %maximum_maximum_fusion.1), channel_id=1, source_target_pairs={{0,16},{16,32},{32,48},{48,64},{64,80},{80,96},{96,112},{112,128},... | collective-permute-start | bytes 6291464 | tf_op jit(solution)/shard_map/ppermute | solution.py:9
  322.5 75.7 %collective-permute-start.4 = (f32[2,5,5,32,512]{4,3,2,1,0:T(8,128)}, f32[2,5,5,32,512]{4,3,2,1,0:T(8,128)}, u32[]{:S(2)}, u32[]{:S(2)}) collective-permute-start(f32[2,5,5,32,512]{4,3,2,1,0:T(8,128)} %maximum_maximum_fusion), channel_id=1, source_target_pairs={{0,16},{16,32},{32,48},{48,64},{64,80},{80,96},{96,112},{112,128},... | collective-permute-start | bytes 9830408 | tf_op jit(solution)/shard_map/ppermute | solution.py:9
  419.4 24.2 %all-to-all-start.4 = ((f32[16,1,10240]{2,1,0:T(1,128)}), f32[16,1,10240]{2,1,0:T(1,128)S(1)}, u32[]{:S(2)}, u32[]{:S(2)}) async-start(f32[16,1,10240]{2,1,0:T(1,128)} %reshape.1607), calls=%async_computation.4 | async-start | bytes 1310720 | tf_op jit(solution)/shard_map/all_to_all | solution.py:13
Sparse Core Ops, SparseCore 0:
  15.9 42.7 all-gather.14
  60.5 38.4 all-gather.6
  100.9 42.6 all-gather.8
  145.3 41.1 all-gather.10
  188.2 47.1 all-gather.12
where the time goes:
time: 474 us; the launch traced here: 466 us
  waiting for transfers between devices  235 us (50%)
  local copies, waits for them, and re-layouts  82.8 us (17%)
  matrix products  40.3 us (9%)
  blocking collectives  39.5 us (8%)
  other arithmetic  35.3 us (7%)
  starting transfers between devices  19.1 us (4%)
  between operations  14.7 us (3%)
    ppermute x5, waiting for transfers between devices, from_behind(): return lax.ppermute(x, axis, [(i, (i + by) % size) for i in range(size)])  174 us
    all_to_all x2, blocking collectives, turn_over(): lax.all_to_all(cross, 'col', split_axis=3, concat_axis=2, tiled=True)  39.5 us
    all_to_all x3, waiting for transfers between devices, turn_over(): lax.all_to_all(cross, 'col', split_axis=3, concat_axis=2, tiled=True)  35.6 us
    all_gather x5, waiting for transfers between devices, shards(): whole = lax.all_gather(lower, 'col', axis=2, tiled=True).astype(jnp.float32)  24.7 us
    unnamed x26, local copies, waits for them, and re-layouts  24.1 us
    all_to_all x11, local copies, waits for them, and re-layouts, turn_over(): lax.all_to_all(cross, 'col', split_axis=3, concat_axis=2, tiled=True)  21.7 us
    dot_general x5, matrix products, shards(): jnp.einsum('nlmik,nmkj->nlij', ancestry, whole, precision=lax.Precision.H...  21.6 us
    dot_general x5, matrix products, shards(): jnp.einsum('nlik,nlkj->nij', turned, whole, precision=lax.Precision.HIGHEST)  18.7 us
  transfers between devices with their start and end apart: 13, of which 10 were waited for; matrix products, arithmetic and copies ran while one was open for 25% of the time, Pallas kernels for 0%

commit v1 on v0

--- a/solution.py
+++ b/solution.py
@@ -2,6 +2,11 @@
 import jax.numpy as jnp
 from jax import lax
 from jax.sharding import PartitionSpec as P
+
+
+def exchange_gather(value, axis, dim):
+    sent = jnp.stack([value] * lax.axis_size(axis))
+    return jnp.concatenate(lax.all_to_all(sent, axis, 0, 0), axis=dim)
 
 
 def from_behind(x, axis, by):
@@ -59,7 +64,7 @@
             start = level * (level - 1) // 2
             keep = (live_upper[:, :, :, None] * live_cols[None, :, None, :]).astype(jnp.bfloat16)
             lower = jnp.transpose(panel[start : start + level] * keep, (1, 0, 2, 3))
-            whole = lax.all_gather(lower, "col", axis=2, tiled=True).astype(jnp.float32)
+            whole = exchange_gather(lower, "col", 2).astype(jnp.float32)
             cross = -jnp.einsum(
                 "nlmik,nmkj->nlij", ancestry, whole, precision=lax.Precision.HIGHEST
             )

time: 474 us -> 602 us (1.27)
  waiting for transfers between devices: 235 us -> 340 us
  starting transfers between devices: 19.1 us -> 60.1 us
  blocking collectives: 39.5 us -> 0 us
  local copies, waits for them, and re-layouts: 82.8 us -> 119 us
  between operations: 14.7 us -> 1.38 us
  matrix products: 40.3 us -> 33.8 us
    all_to_all x0 -> x5, waiting for transfers between devices: none -> 230 us  [exchange_gather(): return jnp.concatenate(lax.all_to_all(sent, axis, 0, 0), axis=dim)]
    ppermute x5, waiting for transfers between devices: 174 us -> 48.6 us  [from_behind(): return lax.ppermute(x, axis, [(i, (i + by) % size) for i in range(size)])]
    all_to_all x2 -> x0, blocking collectives: 39.5 us -> none  [turn_over(): lax.all_to_all(cross, 'col', split_axis=3, concat_axis=2, tiled=True)]
    all_to_all x0 -> x5, starting transfers between devices: none -> 28.3 us  [exchange_gather(): return jnp.concatenate(lax.all_to_all(sent, axis, 0, 0), axis=dim)]
    all_to_all x3 -> x5, waiting for transfers between devices: 35.6 us -> 60.8 us  [turn_over(): lax.all_to_all(cross, 'col', split_axis=3, concat_axis=2, tiled=True)]
    all_gather x5 -> x0, waiting for transfers between devices: 24.7 us -> none  [shards(): whole = lax.all_gather(lower, 'col', axis=2, tiled=True).astype(jnp.float32)]
    reshape x0 -> x5, local copies, waits for them, and re-layouts: none -> 14.7 us  [exchange_gather(): return jnp.concatenate(lax.all_to_all(sent, axis, 0, 0), axis=dim)]
    all_to_all x3 -> x5, starting transfers between devices: 13.5 us -> 25 us  [turn_over(): lax.all_to_all(cross, 'col', split_axis=3, concat_axis=2, tiled=True)]
  transfers between devices with their start and end apart: 13 -> 15, of which waited for: 10 -> 13; matrix products, arithmetic and copies ran while one was open for 25% -> 14% of each run, Pallas kernels for 0% -> 0%
where the time goes in v1:
time: 602 us; the launch traced here: 593 us
  waiting for transfers between devices  340 us (56%)
  local copies, waits for them, and re-layouts  119 us (20%)
  starting transfers between devices  60.1 us (10%)
  other arithmetic  39.3 us (7%)
  matrix products  33.8 us (6%)
    all_to_all x5, waiting for transfers between devices, exchange_gather(): return jnp.concatenate(lax.all_to_all(sent, axis, 0, 0), axis=dim)  230 us
    all_to_all x5, waiting for transfers between devices, turn_over(): lax.all_to_all(cross, 'col', split_axis=3, concat_axis=2, tiled=True)  60.8 us
    ppermute x5, waiting for transfers between devices, from_behind(): return lax.ppermute(x, axis, [(i, (i + by) % size) for i in range(size)])  48.6 us
    unnamed x54, local copies, waits for them, and re-layouts  30.4 us
    all_to_all x5, starting transfers between devices, exchange_gather(): return jnp.concatenate(lax.all_to_all(sent, axis, 0, 0), axis=dim)  28.3 us
    all_to_all x5, starting transfers between devices, turn_over(): lax.all_to_all(cross, 'col', split_axis=3, concat_axis=2, tiled=True)  25 us
    all_to_all x11, local copies, waits for them, and re-layouts, turn_over(): lax.all_to_all(cross, 'col', split_axis=3, concat_axis=2, tiled=True)  23.7 us
    dot_general x5, matrix products, shards(): jnp.einsum('nlik,nlkj->nij', turned, whole, precision=lax.Precision.HIGHEST)  18 us
  transfers between devices with their start and end apart: 15, of which 13 were waited for; matrix products, arithmetic and copies ran while one was open for 14% of the time, Pallas kernels for 0%

profile of v1, /device:TPU:1, one launch (start us, length us, event | category | flops | bytes accessed | tf_op | source)
XLA Modules:
  0.0 593.3 jit_solution(4759252900282844543)
XLA Ops:
  10.1 10.0 %all-to-all-start = ((bf16[16,2,1,32,512]{4,3,1,2,0:T(8,128)(2,1)}), bf16[16,2,1,32,512]{4,3,1,2,0:T(8,128)(2,1)S(1)}, u32[]{:S(2)}, u32[]{:S(2)}) async-start(bf16[16,2,1,32,512]{4,3,1,2,0:T(8,128)(2,1)} %stack.22), calls=%async_computation | async-start | bytes 2097152 | tf_op jit(solution)/shard_map/all_to_all | solution.py:9
  25.2 4.4 collective-permute-done
  30.2 17.9 %all-to-all-done = bf16[16,2,1,32,512]{4,3,1,2,0:T(8,128)(2,1)S(1)} async-done(((bf16[16,2,1,32,512]{4,3,1,2,0:T(8,128)(2,1)}), bf16[16,2,1,32,512]{4,3,1,2,0:T(8,128)(2,1)S(1)}, u32[]{:S(2)}, u32[]{:S(2)}) %all-to-all-start) | async-done | bytes 1048608 | tf_op jit(solution)/shard_map/all_to_all | solution.py:9
  50.9 3.4 all-to-all-start.1
  55.5 7.8 %all-to-all-done.1 = f32[16,1,2048]{2,1,0:T(1,128)S(1)} async-done(((f32[16,1,2048]{2,1,0:T(1,128)}), f32[16,1,2048]{2,1,0:T(1,128)S(1)}, u32[]{:S(2)}, u32[]{:S(2)}) %all-to-all-start.1) | async-done | bytes 131104 | tf_op jit(solution)/shard_map/all_to_all | solution.py:18
  64.8 4.3 all-to-all-start.2
  77.2 15.9 %collective-permute-done.1 = f32[2,2,2,32,512]{4,3,0,2,1:T(8,128)S(1)} collective-permute-done((f32[2,2,2,32,512]{4,3,0,2,1:T(8,128)S(1)}, f32[2,2,2,32,512]{4,3,0,2,1:T(8,128)S(1)}, u32[]{:S(2)}, u32[]{:S(2)}) %collective-permute-start.1) | collective-permute-done | bytes 524320 | tf_op jit(solution)/shard_map/ppermute | solution.py:14
  94.0 24.1 %all-to-all-done.2 = bf16[16,2,2,32,512]{4,3,2,1,0:T(8,128)(2,1)} async-done(((bf16[16,2,2,32,512]{4,3,2,1,0:T(8,128)(2,1)}), bf16[16,2,2,32,512]{4,3,2,1,0:T(8,128)(2,1)}, u32[]{:S(2)}, u32[]{:S(2)}) %all-to-all-start.2) | async-done | bytes 2097184 | tf_op jit(solution)/shard_map/all_to_all | solution.py:9
  122.9 3.0 reshape.1650
  126.0 4.8 all-to-all-start.3
  132.9 9.5 %all-to-all-done.3 = f32[16,1,4096]{2,1,0:T(1,128)S(1)} async-done(((f32[16,1,4096]{2,1,0:T(1,128)}), f32[16,1,4096]{2,1,0:T(1,128)S(1)}, u32[]{:S(2)}, u32[]{:S(2)}) %all-to-all-start.3) | async-done | bytes 262176 | tf_op jit(solution)/shard_map/all_to_all | solution.py:18
  144.5 4.6 all-to-all-start.4
  162.7 28.3 %collective-permute-done.2 = f32[2,3,3,32,512]{4,3,2,1,0:T(8,128)} collective-permute-done((f32[2,3,3,32,512]{4,3,2,1,0:T(8,128)S(1)}, f32[2,3,3,32,512]{4,3,2,1,0:T(8,128)}, u32[]{:S(2)}, u32[]{:S(2)}) %collective-permute-start.2) | collective-permute-done | bytes 1179680 | tf_op jit(solution)/shard_map/ppermute | solution.py:14
  191.0 3.1 pad_maximum_fusion.2
  197.7 21.9 %all-to-all-done.4 = bf16[16,2,3,32,512]{4,3,2,1,0:T(8,128)(2,1)} async-done(((bf16[16,2,3,32,512]{4,3,2,1,0:T(8,128)(2,1)}), bf16[16,2,3,32,512]{4,3,2,1,0:T(8,128)(2,1)}, u32[]{:S(2)}, u32[]{:S(2)}) %all-to-all-start.4) | async-done | bytes 3145760 | tf_op jit(solution)/shard_map/all_to_all | solution.py:9
  224.3 3.1 copy.155
  227.4 3.7 reshape.1652
  231.2 5.5 all-to-all-start.5
  238.8 12.4 %all-to-all-done.5 = f32[16,1,6144]{2,1,0:T(1,128)} async-done(((f32[16,1,6144]{2,1,0:T(1,128)}), f32[16,1,6144]{2,1,0:T(1,128)}, u32[]{:S(2)}, u32[]{:S(2)}) %all-to-all-start.5) | async-done | bytes 393248 | tf_op jit(solution)/shard_map/all_to_all | solution.py:18
  253.8 4.7 all-to-all-start.6
  258.4 3.4 reduce.8
  261.8 3.5 reshape.1653
  265.3 3.5 copy.198
  271.6 3.4 bitcast_dynamic-update-slice_fusion.6
  277.9 73.1 %all-to-all-done.6 = bf16[16,2,4,32,512]{4,3,2,1,0:T(8,128)(2,1)} async-done(((bf16[16,2,4,32,512]{4,3,2,1,0:T(8,128)(2,1)}), bf16[16,2,4,32,512]{4,3,2,1,0:T(8,128)(2,1)}, u32[]{:S(2)}, u32[]{:S(2)}) %all-to-all-start.6) | async-done | bytes 4194336 | tf_op jit(solution)/shard_map/all_to_all | solution.py:9
  351.0 5.0 copy.160
  356.0 4.2 pad_maximum_fusion.1
  360.2 4.2 gather_fusion.18
  371.7 3.5 reshape.1654
  375.2 5.5 all-to-all-start.7
  383.6 14.3 %all-to-all-done.7 = f32[16,1,8192]{2,1,0:T(1,128)S(1)} async-done(((f32[16,1,8192]{2,1,0:T(1,128)}), f32[16,1,8192]{2,1,0:T(1,128)S(1)}, u32[]{:S(2)}, u32[]{:S(2)}) %all-to-all-start.7) | async-done | bytes 524320 | tf_op jit(solution)/shard_map/all_to_all | solution.py:18
  397.9 3.0 stack.26
  401.0 4.7 all-to-all-start.8
  411.1 4.2 copy.197
  417.6 4.9 bitcast_dynamic-update-slice_fusion.5
  427.1 93.3 %all-to-all-done.8 = bf16[16,2,5,32,512]{4,3,2,1,0:T(8,128)(2,1)} async-done(((bf16[16,2,5,32,512]{4,3,2,1,0:T(8,128)(2,1)}), bf16[16,2,5,32,512]{4,3,2,1,0:T(8,128)(2,1)}, u32[]{:S(2)}, u32[]{:S(2)}) %all-to-all-start.8) | async-done | bytes 5242912 | tf_op jit(solution)/shard_map/all_to_all | solution.py:9
  520.4 5.7 copy.166
  526.0 4.7 pad_maximum_fusion
  530.7 5.3 gather_fusion.24
  536.0 7.3 %bitcast_dynamic-update-slice_fusion = (f32[15,2,32,512]{3,2,0,1:T(8,128)}, f32[2,5,32,512]{3,2,1,0:T(8,128)}) fusion(f32[15,2,32,512]{3,2,0,1:T(8,128)} %get-tuple-element.50, bf16[2,5,512,512,1]{3,2,1,4,0:T(8,128)(2,1)} %bitcast.403, f32[2,5,5,32,512]{4,3,2,1,0:T(8,128)} %gather_fusion.24, pred[2]{0:T(512)(128)(4,1)S(1)} %compare_and_fusion), kind=kOutput, calls=%fused_computation.67 | convolution fusion | flops 5034147840 | bytes 9830402 | tf_op jit(solution)/shard_map/nlmik,nmkj->nlij/dot_general | solution.py:68
  543.4 3.1 copy.168
  546.4 3.4 reshape.1656
  549.8 5.8 all-to-all-start.9
  555.6 3.1 copy.170
  558.7 16.8 %all-to-all-done.9 = f32[16,1,10240]{2,1,0:T(1,128)S(1)} async-done(((f32[16,1,10240]{2,1,0:T(1,128)}), f32[16,1,10240]{2,1,0:T(1,128)S(1)}, u32[]{:S(2)}, u32[]{:S(2)}) %all-to-all-start.9) | async-done | bytes 655392 | tf_op jit(solution)/shard_map/all_to_all | solution.py:18
  575.4 3.2 reduce.10
  578.6 3.3 reshape.1657
  587.4 5.7 fusion.17
  (190 shorter events, 98.6 us)
Async XLA Ops:
  0.6 6.1 %copy-start = (s32[6,32]{1,0:T(8,128)S(1)}, s32[6,32]{1,0:T(8,128)}, u32[]{:S(2)}) copy-start(s32[6,32]{1,0:T(8,128)} %param.7) | copy-start | bytes 2308
  0.6 4.9 copy-start.16
  1.6 379.2 %copy-start.11 = (s32[1024]{0:T(1024)}, s32[1024]{0:T(1024)S(1)}, u32[]{:S(2)}) copy-start(s32[1024]{0:T(1024)S(1)} %pad_clamp_fusion.9) | copy-start | bytes 12292
  5.5 15.4 %copy-start.10 = (f32[6,2,32,512]{3,2,1,0:T(8,128)S(1)}, f32[6,2,32,512]{3,2,1,0:T(8,128)}, u32[]{:S(2)}) copy-start(f32[6,2,32,512]{3,2,1,0:T(8,128)} %param.5) | copy-start | bytes 2359300
  10.1 38.0 %all-to-all-start = ((bf16[16,2,1,32,512]{4,3,1,2,0:T(8,128)(2,1)}), bf16[16,2,1,32,512]{4,3,1,2,0:T(8,128)(2,1)S(1)}, u32[]{:S(2)}, u32[]{:S(2)}) async-start(bf16[16,2,1,32,512]{4,3,1,2,0:T(8,128)(2,1)} %stack.22), calls=%async_computation | async-start | bytes 2097152 | tf_op jit(solution)/shard_map/all_to_all | solution.py:9
  20.9 8.6 %collective-permute-start = (f32[2,1,1,32,512]{4,3,0,2,1:T(8,128)S(1)}, f32[2,1,1,32,512]{4,3,0,2,1:T(8,128)S(1)}, u32[]{:S(2)}, u32[]{:S(2)}) collective-permute-start(f32[2,1,1,32,512]{4,3,0,2,1:T(8,128)S(1)} %fusion.43), channel_id=1, source_target_pairs={{0,16},{16,32},{32,48},{48,64},{64,80},{80,96},{96,112},{112,128},... | collective-permute-start | bytes 393224 | tf_op jit(solution)/shard_map/ppermute | solution.py:14
  50.9 12.3 %all-to-all-start.1 = ((f32[16,1,2048]{2,1,0:T(1,128)}), f32[16,1,2048]{2,1,0:T(1,128)S(1)}, u32[]{:S(2)}, u32[]{:S(2)}) async-start(f32[16,1,2048]{2,1,0:T(1,128)} %reshape.1648), calls=%async_computation.1 | async-start | bytes 262144 | tf_op jit(solution)/shard_map/all_to_all | solution.py:18
  64.8 53.2 %all-to-all-start.2 = ((bf16[16,2,2,32,512]{4,3,2,1,0:T(8,128)(2,1)}), bf16[16,2,2,32,512]{4,3,2,1,0:T(8,128)(2,1)}, u32[]{:S(2)}, u32[]{:S(2)}) async-start(bf16[16,2,2,32,512]{4,3,2,1,0:T(8,128)(2,1)} %stack.23), calls=%async_computation.2 | async-start | bytes 4194304 | tf_op jit(solution)/shard_map/all_to_all | solution.py:9
  75.9 17.3 %collective-permute-start.1 = (f32[2,2,2,32,512]{4,3,0,2,1:T(8,128)S(1)}, f32[2,2,2,32,512]{4,3,0,2,1:T(8,128)S(1)}, u32[]{:S(2)}, u32[]{:S(2)}) collective-permute-start(f32[2,2,2,32,512]{4,3,0,2,1:T(8,128)S(1)} %maximum_maximum_fusion.3), channel_id=1, source_target_pairs={{0,16},{16,32},{32,48},{48,64},{64,80},{80,96},{96,112},{112,128},... | collective-permute-start | bytes 1572872 | tf_op jit(solution)/shard_map/ppermute | solution.py:14
  126.0 16.4 %all-to-all-start.3 = ((f32[16,1,4096]{2,1,0:T(1,128)}), f32[16,1,4096]{2,1,0:T(1,128)S(1)}, u32[]{:S(2)}, u32[]{:S(2)}) async-start(f32[16,1,4096]{2,1,0:T(1,128)} %reshape.1650), calls=%async_computation.3 | async-start | bytes 524288 | tf_op jit(solution)/shard_map/all_to_all | solution.py:18
  144.5 75.1 %all-to-all-start.4 = ((bf16[16,2,3,32,512]{4,3,2,1,0:T(8,128)(2,1)}), bf16[16,2,3,32,512]{4,3,2,1,0:T(8,128)(2,1)}, u32[]{:S(2)}, u32[]{:S(2)}) async-start(bf16[16,2,3,32,512]{4,3,2,1,0:T(8,128)(2,1)} %stack.24), calls=%async_computation.4 | async-start | bytes 6291456 | tf_op jit(solution)/shard_map/all_to_all | solution.py:9
  156.6 4.7 copy-start.17
  156.6 4.8 copy-start.18
  156.7 4.8 copy-start.19
  159.5 31.6 %collective-permute-start.2 = (f32[2,3,3,32,512]{4,3,2,1,0:T(8,128)S(1)}, f32[2,3,3,32,512]{4,3,2,1,0:T(8,128)}, u32[]{:S(2)}, u32[]{:S(2)}) collective-permute-start(f32[2,3,3,32,512]{4,3,2,1,0:T(8,128)S(1)} %maximum_maximum_fusion.2), channel_id=1, source_target_pairs={{0,16},{16,32},{32,48},{48,64},{64,80},{80,96},{96,112},{112,128},... | collective-permute-start | bytes 3538952 | tf_op jit(solution)/shard_map/ppermute | solution.py:14
  219.5 2.2 copy-start.1
  231.2 20.1 %all-to-all-start.5 = ((f32[16,1,6144]{2,1,0:T(1,128)}), f32[16,1,6144]{2,1,0:T(1,128)}, u32[]{:S(2)}, u32[]{:S(2)}) async-start(f32[16,1,6144]{2,1,0:T(1,128)} %reshape.1652), calls=%async_computation.5 | async-start | bytes 786432 | tf_op jit(solution)/shard_map/all_to_all | solution.py:18
  253.8 97.2 %all-to-all-start.6 = ((bf16[16,2,4,32,512]{4,3,2,1,0:T(8,128)(2,1)}), bf16[16,2,4,32,512]{4,3,2,1,0:T(8,128)(2,1)}, u32[]{:S(2)}, u32[]{:S(2)}) async-start(bf16[16,2,4,32,512]{4,3,2,1,0:T(8,128)(2,1)} %stack.25), calls=%async_computation.6 | async-start | bytes 8388608 | tf_op jit(solution)/shard_map/all_to_all | solution.py:9
  271.6 3.4 copy-start.2
  271.6 3.4 copy-start.5
  271.6 3.4 copy-start.7
  275.3 80.7 %collective-permute-start.3 = (f32[2,4,4,32,512]{4,3,2,1,0:T(8,128)S(1)}, f32[2,4,4,32,512]{4,3,2,1,0:T(8,128)}, u32[]{:S(2)}, u32[]{:S(2)}) collective-permute-start(f32[2,4,4,32,512]{4,3,2,1,0:T(8,128)S(1)} %maximum_maximum_fusion.1), channel_id=1, source_target_pairs={{0,16},{16,32},{32,48},{48,64},{64,80},{80,96},{96,112},{112,128},... | collective-permute-start | bytes 6291464 | tf_op jit(solution)/shard_map/ppermute | solution.py:14
  351.0 5.0 copy-start.3
  351.0 5.0 copy-start.6
  351.0 5.0 copy-start.8
  364.4 2.8 copy-start.4
  375.2 22.7 %all-to-all-start.7 = ((f32[16,1,8192]{2,1,0:T(1,128)}), f32[16,1,8192]{2,1,0:T(1,128)S(1)}, u32[]{:S(2)}, u32[]{:S(2)}) async-start(f32[16,1,8192]{2,1,0:T(1,128)} %reshape.1654), calls=%async_computation.7 | async-start | bytes 1048576 | tf_op jit(solution)/shard_map/all_to_all | solution.py:18
  397.9 3.0 copy-start.9
  401.0 119.4 %all-to-all-start.8 = ((bf16[16,2,5,32,512]{4,3,2,1,0:T(8,128)(2,1)}), bf16[16,2,5,32,512]{4,3,2,1,0:T(8,128)(2,1)}, u32[]{:S(2)}, u32[]{:S(2)}) async-start(bf16[16,2,5,32,512]{4,3,2,1,0:T(8,128)(2,1)} %stack.26), calls=%async_computation.8 | async-start | bytes 10485760 | tf_op jit(solution)/shard_map/all_to_all | solution.py:9
  415.3 2.3 copy-start.12
  415.3 2.3 copy-start.13
  424.6 101.4 %collective-permute-start.4 = (f32[2,5,5,32,512]{4,3,2,1,0:T(8,128)}, f32[2,5,5,32,512]{4,3,2,1,0:T(8,128)}, u32[]{:S(2)}, u32[]{:S(2)}) collective-permute-start(f32[2,5,5,32,512]{4,3,2,1,0:T(8,128)} %maximum_maximum_fusion), channel_id=1, source_target_pairs={{0,16},{16,32},{32,48},{48,64},{64,80},{80,96},{96,112},{112,128},... | collective-permute-start | bytes 9830408 | tf_op jit(solution)/shard_map/ppermute | solution.py:14
  549.8 25.6 %all-to-all-start.9 = ((f32[16,1,10240]{2,1,0:T(1,128)}), f32[16,1,10240]{2,1,0:T(1,128)S(1)}, u32[]{:S(2)}, u32[]{:S(2)}) async-start(f32[16,1,10240]{2,1,0:T(1,128)} %reshape.1656), calls=%async_computation.9 | async-start | bytes 1310720 | tf_op jit(solution)/shard_map/all_to_all | solution.py:18
  584.9 2.5 copy-start.14
  584.9 2.5 copy-start.15
